TPU v7x, 128 devices: a whole 4x4x4 slice. The times are simulated.
128 devices in a mesh: rows: 16 (over x, z), cols: 8 (over y, core).
Axes of the slice: x: 4, y: 4, z: 4, core: 2. Of those that a mesh axis runs over, the one named last changes fastest.
Arguments:
- panel_cols: bfloat16 [64, 32, 256, 128], P('rows', 'cols'), may hold values from -1.75 to 1.75
- pivot_inv: bfloat16 [32, 256, 256], P('cols'), may hold values from -0.375 to 0.375
- pivot_rows: bfloat16 [32, 48, 256, 128], P('rows', 'cols'), may hold values from -1.75 to 1.75
- target_factors: bfloat16 [64, 48, 256, 128], P('rows', 'cols'), may hold values from -5 to 5
- near_blocks: bfloat16 [64, 8, 256, 256], P('rows', 'cols'), may hold values from -6 to 6
- near_cols: int32 [64, 8], P('rows', 'cols'), may hold values from 0 to 5, as said below
- sketch: bfloat16 [48, 256, 64], P('cols'), may hold values from -6 to 6
Outputs:
- near_out: bfloat16 [64, 8, 256, 256], P('rows', 'cols')
- far_out: bfloat16 [64, 48, 256, 128], P('rows', 'cols')
Inputs may be any that keep to these rules, and one draw needn't show every extreme that they name: `near_cols`: for every block row, the 1 entries of each group of slots s with equal s // 1 are distinct.
All inputs are finite; a program needn't handle non-finite values.
Results may differ from a plain program's by a relative error of at most 0.009.
Values may be sent and summed in bfloat16 or wider, within the bound.
A program may use at most 128 MiB of HBM per device.

v0:
```python
import math

import jax
import jax.numpy as jnp
from jax import lax
from jax.sharding import PartitionSpec as P


def spread(block, axis, holder):
    block = jnp.where(lax.axis_index(axis) == holder, block, jnp.zeros_like(block))
    return lax.psum(block, axis)


def product_of(form, left, right):
    return jnp.einsum(form, left, right, preferred_element_type=jnp.float32)


def row_update(left_row, rows_all, target_row, near_row, near_index, sketch):
    half = left_row.shape[-1] // 2
    root_size = math.sqrt(left_row.shape[1])
    left_x = left_row[..., :half]
    left_y = left_row[..., half:]
    pivot_p = rows_all[..., :half]
    pivot_q = rows_all[..., half:]
    mid_cores = product_of("kbr,kjbs->kjrs", left_y, pivot_p).astype(jnp.bfloat16)
    left_terms = product_of("kbr,kjrs->jkbs", left_x, mid_cores).astype(jnp.bfloat16)
    left_near = jnp.take(left_terms, near_index, axis=0)
    q_near = jnp.take(pivot_q, near_index, axis=1)
    update = product_of("nkbs,kncs->nbc", left_near, q_near)
    near_new = (near_row.astype(jnp.float32) - update).astype(jnp.bfloat16)
    column_ids = jnp.arange(target_row.shape[0], dtype=jnp.int32)
    is_near = jnp.any(near_index[:, None] == column_ids[None, :], axis=0)
    target_u = target_row[..., :half]
    target_v = target_row[..., half:]
    sketch_core = product_of("jbs,jbt->jst", target_v, sketch).astype(jnp.bfloat16)
    pivot_sketch = product_of("kjbs,jbt->jkst", pivot_q, sketch).astype(jnp.bfloat16)
    sampled = product_of("jbs,jst->jbt", target_u, sketch_core) - product_of(
        "jkbs,jkst->jbt", left_terms, pivot_sketch
    )
    gram_matrix = jnp.einsum("jbs,jbt->jst", sampled, sampled, precision=lax.Precision.HIGHEST)
    factor_chol = jnp.linalg.cholesky(gram_matrix)
    orthonormal = lax.linalg.triangular_solve(
        factor_chol, sampled, left_side=False, lower=True, transpose_a=True
    )
    basis = (root_size * orthonormal).astype(jnp.bfloat16)
    basis_core = product_of("jbs,jbt->jst", target_u, basis).astype(jnp.bfloat16)
    left_core = product_of("jkbs,jbt->jkst", left_terms, basis).astype(jnp.bfloat16)
    weights_out = (
        product_of("jbs,jst->jbt", target_v, basis_core)
        - product_of("kjbs,jkst->jbt", pivot_q, left_core)
    ) / root_size
    keep_far = jnp.where(is_near, 0.0, 1.0).astype(jnp.bfloat16)[:, None, None]
    far_new = jnp.concatenate([basis, weights_out.astype(jnp.bfloat16)], axis=-1) * keep_far
    return (near_new, far_new)


def per_device(panel_cols, pivot_inv, pivot_rows, target_factors, near_blocks, near_cols, sketch):
    half = panel_cols.shape[-1] // 2
    col_left = panel_cols[..., :half]
    col_right = panel_cols[..., half:]
    pivot_right = product_of("kab,ikar->ikbr", pivot_inv, col_right).astype(jnp.bfloat16)
    local_panel = jnp.concatenate([col_left, pivot_right], axis=-1)
    panel_all = lax.all_gather(local_panel, "cols", axis=1, tiled=True)
    owned = pivot_rows.shape[0]
    row_count = lax.axis_size("rows")

    def fetch(owner, buffer):
        arrived = spread(pivot_rows, "rows", owner)
        return lax.dynamic_update_slice_in_dim(
            buffer, arrived, (owner * owned).astype(jnp.int32), 0
        )

    empty = jnp.zeros((row_count * owned,) + pivot_rows.shape[1:], jnp.bfloat16)
    rows_all = lax.fori_loop(0, row_count, fetch, empty)

    def one_row(row_items):
        return row_update(row_items[0], rows_all, row_items[1], row_items[2], row_items[3], sketch)

    near_new, far_new = lax.map(one_row, (panel_all, target_factors, near_blocks, near_cols))
    return (near_new, far_new)


def solution(mesh):
    placed = (
        P("rows", "cols", None, None),
        P("cols", None, None),
        P("rows", "cols", None, None),
        P("rows", "cols", None, None),
        P("rows", "cols", None, None),
        P("rows", "cols"),
        P("cols", None, None),
    )
    return jax.shard_map(
        per_device,
        mesh=mesh,
        in_specs=placed,
        out_specs=(P("rows", "cols", None, None), P("rows", "cols", None, None)),
        check_vma=False,
    )
```

profile of v0, /device:TPU:1, one launch (start us, length us, event | category | flops | bytes accessed | tf_op | source)
XLA Modules:
  0.0 2002.7 jit_solution(16693872794983531070)
XLA Ops:
  20.1 1473.8 %while.29 = (s32[]{:T(128)}, bf16[32,6,256,128]{3,2,1,0:T(8,128)(2,1)}, bf16[2,6,256,128]{3,2,1,0:T(8,128)(2,1)S(1)}, s32[]{:T(128)}, u32[]{:T(128)}, /*index=5*/u32[]{:T(128)}, s32[]{:T(128)}, s32[]{:T(128)}, s32[]{:T(128)}) while((s32[]{:T(128)}, bf16[32,6,256,128]{3,2,1,0:T(8,128)(2,1)}, bf16[2,6,256,128]{3,2,1,0:T(8,128)(2,1)S(1)}, ...), condition=%wide.region_2.3_spmd, body=%wide.region_0.2_spmd.sunk | while | flops 786442 | bytes 7864545 | solution.py:74
  21.1 91.7 %all-reduce.2.cloned.1.call-done = bf16[2,6,256,128]{3,2,1,0:T(8,128)(2,1)} async-done(((bf16[2,6,256,128]{3,2,1,0:T(8,128)(2,1)}), bf16[2,6,256,128]{3,2,1,0:T(8,128)(2,1)}) %all-reduce.2.cloned.1.call-update) | async-done | bytes 786448 | tf_op jit(solution)/shard_map/while/body/eval_jaxpr/psum | solution.py:11
  115.9 89.1 %all-reduce.2.cloned.1.call-done = bf16[2,6,256,128]{3,2,1,0:T(8,128)(2,1)} async-done(((bf16[2,6,256,128]{3,2,1,0:T(8,128)(2,1)}), bf16[2,6,256,128]{3,2,1,0:T(8,128)(2,1)}) %all-reduce.2.cloned.1.call-update) | async-done | bytes 786448 | tf_op jit(solution)/shard_map/while/body/eval_jaxpr/psum | solution.py:11
  207.9 89.1 %all-reduce.2.cloned.1.call-done = bf16[2,6,256,128]{3,2,1,0:T(8,128)(2,1)} async-done(((bf16[2,6,256,128]{3,2,1,0:T(8,128)(2,1)}), bf16[2,6,256,128]{3,2,1,0:T(8,128)(2,1)}) %all-reduce.2.cloned.1.call-update) | async-done | bytes 786448 | tf_op jit(solution)/shard_map/while/body/eval_jaxpr/psum | solution.py:11
  300.0 88.7 %all-reduce.2.cloned.1.call-done = bf16[2,6,256,128]{3,2,1,0:T(8,128)(2,1)} async-done(((bf16[2,6,256,128]{3,2,1,0:T(8,128)(2,1)}), bf16[2,6,256,128]{3,2,1,0:T(8,128)(2,1)}) %all-reduce.2.cloned.1.call-update) | async-done | bytes 786448 | tf_op jit(solution)/shard_map/while/body/eval_jaxpr/psum | solution.py:11
  391.8 88.7 %all-reduce.2.cloned.1.call-done = bf16[2,6,256,128]{3,2,1,0:T(8,128)(2,1)} async-done(((bf16[2,6,256,128]{3,2,1,0:T(8,128)(2,1)}), bf16[2,6,256,128]{3,2,1,0:T(8,128)(2,1)}) %all-reduce.2.cloned.1.call-update) | async-done | bytes 786448 | tf_op jit(solution)/shard_map/while/body/eval_jaxpr/psum | solution.py:11
  483.6 88.7 %all-reduce.2.cloned.1.call-done = bf16[2,6,256,128]{3,2,1,0:T(8,128)(2,1)} async-done(((bf16[2,6,256,128]{3,2,1,0:T(8,128)(2,1)}), bf16[2,6,256,128]{3,2,1,0:T(8,128)(2,1)}) %all-reduce.2.cloned.1.call-update) | async-done | bytes 786448 | tf_op jit(solution)/shard_map/while/body/eval_jaxpr/psum | solution.py:11
  575.4 89.1 %all-reduce.2.cloned.1.call-done = bf16[2,6,256,128]{3,2,1,0:T(8,128)(2,1)} async-done(((bf16[2,6,256,128]{3,2,1,0:T(8,128)(2,1)}), bf16[2,6,256,128]{3,2,1,0:T(8,128)(2,1)}) %all-reduce.2.cloned.1.call-update) | async-done | bytes 786448 | tf_op jit(solution)/shard_map/while/body/eval_jaxpr/psum | solution.py:11
  667.5 89.1 %all-reduce.2.cloned.1.call-done = bf16[2,6,256,128]{3,2,1,0:T(8,128)(2,1)} async-done(((bf16[2,6,256,128]{3,2,1,0:T(8,128)(2,1)}), bf16[2,6,256,128]{3,2,1,0:T(8,128)(2,1)}) %all-reduce.2.cloned.1.call-update) | async-done | bytes 786448 | tf_op jit(solution)/shard_map/while/body/eval_jaxpr/psum | solution.py:11
  759.6 89.1 %all-reduce.2.cloned.1.call-done = bf16[2,6,256,128]{3,2,1,0:T(8,128)(2,1)} async-done(((bf16[2,6,256,128]{3,2,1,0:T(8,128)(2,1)}), bf16[2,6,256,128]{3,2,1,0:T(8,128)(2,1)}) %all-reduce.2.cloned.1.call-update) | async-done | bytes 786448 | tf_op jit(solution)/shard_map/while/body/eval_jaxpr/psum | solution.py:11
  851.7 88.7 %all-reduce.2.cloned.1.call-done = bf16[2,6,256,128]{3,2,1,0:T(8,128)(2,1)} async-done(((bf16[2,6,256,128]{3,2,1,0:T(8,128)(2,1)}), bf16[2,6,256,128]{3,2,1,0:T(8,128)(2,1)}) %all-reduce.2.cloned.1.call-update) | async-done | bytes 786448 | tf_op jit(solution)/shard_map/while/body/eval_jaxpr/psum | solution.py:11
  943.5 89.1 %all-reduce.2.cloned.1.call-done = bf16[2,6,256,128]{3,2,1,0:T(8,128)(2,1)} async-done(((bf16[2,6,256,128]{3,2,1,0:T(8,128)(2,1)}), bf16[2,6,256,128]{3,2,1,0:T(8,128)(2,1)}) %all-reduce.2.cloned.1.call-update) | async-done | bytes 786448 | tf_op jit(solution)/shard_map/while/body/eval_jaxpr/psum | solution.py:11
  1035.6 88.7 %all-reduce.2.cloned.1.call-done = bf16[2,6,256,128]{3,2,1,0:T(8,128)(2,1)} async-done(((bf16[2,6,256,128]{3,2,1,0:T(8,128)(2,1)}), bf16[2,6,256,128]{3,2,1,0:T(8,128)(2,1)}) %all-reduce.2.cloned.1.call-update) | async-done | bytes 786448 | tf_op jit(solution)/shard_map/while/body/eval_jaxpr/psum | solution.py:11
  1127.4 89.1 %all-reduce.2.cloned.1.call-done = bf16[2,6,256,128]{3,2,1,0:T(8,128)(2,1)} async-done(((bf16[2,6,256,128]{3,2,1,0:T(8,128)(2,1)}), bf16[2,6,256,128]{3,2,1,0:T(8,128)(2,1)}) %all-reduce.2.cloned.1.call-update) | async-done | bytes 786448 | tf_op jit(solution)/shard_map/while/body/eval_jaxpr/psum | solution.py:11
  1219.5 88.7 %all-reduce.2.cloned.1.call-done = bf16[2,6,256,128]{3,2,1,0:T(8,128)(2,1)} async-done(((bf16[2,6,256,128]{3,2,1,0:T(8,128)(2,1)}), bf16[2,6,256,128]{3,2,1,0:T(8,128)(2,1)}) %all-reduce.2.cloned.1.call-update) | async-done | bytes 786448 | tf_op jit(solution)/shard_map/while/body/eval_jaxpr/psum | solution.py:11
  1311.3 88.7 %all-reduce.2.cloned.1.call-done = bf16[2,6,256,128]{3,2,1,0:T(8,128)(2,1)} async-done(((bf16[2,6,256,128]{3,2,1,0:T(8,128)(2,1)}), bf16[2,6,256,128]{3,2,1,0:T(8,128)(2,1)}) %all-reduce.2.cloned.1.call-update) | async-done | bytes 786448 | tf_op jit(solution)/shard_map/while/body/eval_jaxpr/psum | solution.py:11
  1403.1 88.7 %all-reduce.2.cloned.1.call-done = bf16[2,6,256,128]{3,2,1,0:T(8,128)(2,1)} async-done(((bf16[2,6,256,128]{3,2,1,0:T(8,128)(2,1)}), bf16[2,6,256,128]{3,2,1,0:T(8,128)(2,1)}) %all-reduce.2.cloned.1.call-update) | async-done | bytes 786448 | tf_op jit(solution)/shard_map/while/body/eval_jaxpr/psum | solution.py:11
  1494.5 16.8 copy.60
  1511.4 16.6 copy.62
  1546.7 447.8 %while.30 = (s32[]{:T(128)}, bf16[4,1,256,256]{3,2,1,0:T(8,128)(2,1)}, bf16[4,6,256,128]{3,2,1,0:T(8,128)(2,1)}, bf16[4,1,256,256]{3,2,1,0:T(8,128)(2,1)}, s32[4...) while((s32[]{:T(128)}, ...), condition=%wide.region_6.7_spmd, body=%wide.region_3.6_spmd.sunk | while | flops 2490991104 | bytes 93083896 | solution.py:79
  1553.2 10.2 convolution_convert_fusion.5
  1571.4 35.2 %custom-call.15 = f32[6,64,64]{2,1,0:T(8,128)S(1)} custom-call(f32[6,64,64]{2,1,0:T(8,128)S(1)} %fusion.126), custom_call_target="Cholesky" | custom-call | tf_op jit(solution)/shard_map/while/body/eval_jaxpr/jit(cholesky)/cholesky | solution.py:41
  1606.9 29.5 %custom-call.16 = f32[6,1,64,64]{2,3,1,0:T(8,128)S(1)} custom-call(f32[6,1,64,64]{3,2,1,0:T(8,128)S(1)} %select_bitcast_fusion.2), custom_call_target="InvertDiagBlocksLowerTriangular" | custom-call | tf_op jit(solution)/shard_map/while/body/eval_jaxpr/triangular_solve | solution.py:42
  1665.1 10.2 convolution_convert_fusion.5
  1683.4 35.2 %custom-call.15 = f32[6,64,64]{2,1,0:T(8,128)S(1)} custom-call(f32[6,64,64]{2,1,0:T(8,128)S(1)} %fusion.126), custom_call_target="Cholesky" | custom-call | tf_op jit(solution)/shard_map/while/body/eval_jaxpr/jit(cholesky)/cholesky | solution.py:41
  1718.8 29.5 %custom-call.16 = f32[6,1,64,64]{2,3,1,0:T(8,128)S(1)} custom-call(f32[6,1,64,64]{3,2,1,0:T(8,128)S(1)} %select_bitcast_fusion.2), custom_call_target="InvertDiagBlocksLowerTriangular" | custom-call | tf_op jit(solution)/shard_map/while/body/eval_jaxpr/triangular_solve | solution.py:42
  1777.1 10.2 convolution_convert_fusion.5
  1795.3 35.2 %custom-call.15 = f32[6,64,64]{2,1,0:T(8,128)S(1)} custom-call(f32[6,64,64]{2,1,0:T(8,128)S(1)} %fusion.126), custom_call_target="Cholesky" | custom-call | tf_op jit(solution)/shard_map/while/body/eval_jaxpr/jit(cholesky)/cholesky | solution.py:41
  1830.8 29.5 %custom-call.16 = f32[6,1,64,64]{2,3,1,0:T(8,128)S(1)} custom-call(f32[6,1,64,64]{3,2,1,0:T(8,128)S(1)} %select_bitcast_fusion.2), custom_call_target="InvertDiagBlocksLowerTriangular" | custom-call | tf_op jit(solution)/shard_map/while/body/eval_jaxpr/triangular_solve | solution.py:42
  1889.1 10.2 convolution_convert_fusion.5
  1907.3 35.2 %custom-call.15 = f32[6,64,64]{2,1,0:T(8,128)S(1)} custom-call(f32[6,64,64]{2,1,0:T(8,128)S(1)} %fusion.126), custom_call_target="Cholesky" | custom-call | tf_op jit(solution)/shard_map/while/body/eval_jaxpr/jit(cholesky)/cholesky | solution.py:41
  1942.8 29.5 %custom-call.16 = f32[6,1,64,64]{2,3,1,0:T(8,128)S(1)} custom-call(f32[6,1,64,64]{3,2,1,0:T(8,128)S(1)} %select_bitcast_fusion.2), custom_call_target="InvertDiagBlocksLowerTriangular" | custom-call | tf_op jit(solution)/shard_map/while/body/eval_jaxpr/triangular_solve | solution.py:42
  (185 shorter events, 222.1 us)
Async XLA Ops:
  8.0 2.4 copy-start
  12.3 7.8 copy-start.2
  20.1 92.7 %all-reduce.2.cloned.1.call-start = ((), (), s32[]{:S(2)}) async-start(), calls=%async_computation.1 | async-start | bytes 1572864 | tf_op jit(solution)/shard_map/while/body/eval_jaxpr/psum | solution.py:11
  114.9 90.0 %all-reduce.2.cloned.1.call-start = ((), (), s32[]{:S(2)}) async-start(), calls=%async_computation.1 | async-start | bytes 1572864 | tf_op jit(solution)/shard_map/while/body/eval_jaxpr/psum | solution.py:11
  207.0 90.0 %all-reduce.2.cloned.1.call-start = ((), (), s32[]{:S(2)}) async-start(), calls=%async_computation.1 | async-start | bytes 1572864 | tf_op jit(solution)/shard_map/while/body/eval_jaxpr/psum | solution.py:11
  299.1 89.7 %all-reduce.2.cloned.1.call-start = ((), (), s32[]{:S(2)}) async-start(), calls=%async_computation.1 | async-start | bytes 1572864 | tf_op jit(solution)/shard_map/while/body/eval_jaxpr/psum | solution.py:11
  390.9 89.7 %all-reduce.2.cloned.1.call-start = ((), (), s32[]{:S(2)}) async-start(), calls=%async_computation.1 | async-start | bytes 1572864 | tf_op jit(solution)/shard_map/while/body/eval_jaxpr/psum | solution.py:11
  482.6 89.7 %all-reduce.2.cloned.1.call-start = ((), (), s32[]{:S(2)}) async-start(), calls=%async_computation.1 | async-start | bytes 1572864 | tf_op jit(solution)/shard_map/while/body/eval_jaxpr/psum | solution.py:11
  574.4 90.0 %all-reduce.2.cloned.1.call-start = ((), (), s32[]{:S(2)}) async-start(), calls=%async_computation.1 | async-start | bytes 1572864 | tf_op jit(solution)/shard_map/while/body/eval_jaxpr/psum | solution.py:11
  666.5 90.0 %all-reduce.2.cloned.1.call-start = ((), (), s32[]{:S(2)}) async-start(), calls=%async_computation.1 | async-start | bytes 1572864 | tf_op jit(solution)/shard_map/while/body/eval_jaxpr/psum | solution.py:11
  758.6 90.0 %all-reduce.2.cloned.1.call-start = ((), (), s32[]{:S(2)}) async-start(), calls=%async_computation.1 | async-start | bytes 1572864 | tf_op jit(solution)/shard_map/while/body/eval_jaxpr/psum | solution.py:11
  850.7 89.7 %all-reduce.2.cloned.1.call-start = ((), (), s32[]{:S(2)}) async-start(), calls=%async_computation.1 | async-start | bytes 1572864 | tf_op jit(solution)/shard_map/while/body/eval_jaxpr/psum | solution.py:11
  942.5 90.0 %all-reduce.2.cloned.1.call-start = ((), (), s32[]{:S(2)}) async-start(), calls=%async_computation.1 | async-start | bytes 1572864 | tf_op jit(solution)/shard_map/while/body/eval_jaxpr/psum | solution.py:11
  1034.6 89.7 %all-reduce.2.cloned.1.call-start = ((), (), s32[]{:S(2)}) async-start(), calls=%async_computation.1 | async-start | bytes 1572864 | tf_op jit(solution)/shard_map/while/body/eval_jaxpr/psum | solution.py:11
  1126.4 90.0 %all-reduce.2.cloned.1.call-start = ((), (), s32[]{:S(2)}) async-start(), calls=%async_computation.1 | async-start | bytes 1572864 | tf_op jit(solution)/shard_map/while/body/eval_jaxpr/psum | solution.py:11
  1218.5 89.7 %all-reduce.2.cloned.1.call-start = ((), (), s32[]{:S(2)}) async-start(), calls=%async_computation.1 | async-start | bytes 1572864 | tf_op jit(solution)/shard_map/while/body/eval_jaxpr/psum | solution.py:11
  1310.3 89.7 %all-reduce.2.cloned.1.call-start = ((), (), s32[]{:S(2)}) async-start(), calls=%async_computation.1 | async-start | bytes 1572864 | tf_op jit(solution)/shard_map/while/body/eval_jaxpr/psum | solution.py:11
  1402.1 89.7 %all-reduce.2.cloned.1.call-start = ((), (), s32[]{:S(2)}) async-start(), calls=%async_computation.1 | async-start | bytes 1572864 | tf_op jit(solution)/shard_map/while/body/eval_jaxpr/psum | solution.py:11
  1493.9 52.8 %all-gather.2.cloned.1.call-start = ((), (), s32[]{:S(2)}) async-start(), calls=%async_computation | async-start | bytes 9437184 | tf_op jit(solution)/shard_map/all_gather | solution.py:63
  1527.9 18.8 copy-start.3
  1994.6 1.0 copy-start.1
Sparse Core Ops, SparseCore 0:
  24.7 87.9 all-reduce.1
  119.5 85.3 all-reduce.1
  211.6 85.3 all-reduce.1
  303.4 85.3 all-reduce.1
  395.2 85.3 all-reduce.1
  487.0 85.3 all-reduce.1
  579.1 85.3 all-reduce.1
  671.2 85.3 all-reduce.1
  763.3 85.3 all-reduce.1
  855.1 85.3 all-reduce.1
  947.2 85.3 all-reduce.1
  1039.0 85.3 all-reduce.1
  1131.1 85.3 all-reduce.1
  1222.9 85.3 all-reduce.1
  1314.7 85.3 all-reduce.1
  1406.5 85.3 all-reduce.1
Sparse Core Ops, SparseCore 1:
  1496.1 50.6 all-gather.1
where the time goes:
time: 2010 us; the launch traced here: 2000 us
  waiting for transfers between devices  1430 us (71%)
  other arithmetic  278 us (14%)
  local copies, waits for them, and re-layouts  151 us (8%)
  matrix products  118 us (6%)
    psum x16, waiting for transfers between devices, spread(): return lax.psum(block, axis)  1430 us
    another operation x16, other arithmetic, row_update(): factor_chol = jnp.linalg.cholesky(gram_matrix)  141 us
    another operation x12, other arithmetic, row_update(): lax.linalg.triangular_solve(factor_chol, sampled, left_side=False, lower=...  118 us
    dot_general x26, matrix products, product_of(): return jnp.einsum(form, left, right, preferred_element_type=jnp.float32)  114 us
  transfers between devices with their start and end apart: 17, of which 17 were waited for; matrix products, arithmetic and copies ran while one was open for 2% of the time, Pallas kernels for 0%

commit v1 on v0

v1 whole, which is shorter than its diff:
```python
import jax
import jax.numpy as jnp
from jax import lax
from jax.experimental import pallas as pl
from jax.experimental.pallas import tpu as pltpu
from jax.sharding import PartitionSpec as P

MESH = pl.DeviceIdType.MESH
BF = jnp.bfloat16
F32 = jnp.float32
HIGH = lax.Precision.HIGHEST
RING = 4


class Place:
    def __init__(self):
        self.row, self.col = lax.axis_index("rows"), lax.axis_index("cols")
        self.x, self.z = self.row // RING, self.row % RING
        self.y, self.core = self.col // 2, self.col % 2

    def at(self, axis, step):
        if axis == "x":
            return (lax.rem(self.x + step + RING, RING) * RING + self.z, self.col)
        if axis == "z":
            return (self.x * RING + lax.rem(self.z + step + RING, RING), self.col)
        if axis == "y":
            return (self.row, lax.rem(self.y + step + RING, RING) * 2 + self.core)
        return (self.row, self.y * 2 + (1 - self.core))


def row_slot(half, da, db):
    dx, dz = (da, db) if half == 0 else (db, da)
    return (dx % RING) * RING + dz % RING


def offsets(half, slot):
    return slot // RING, slot % RING


def dot_nt(left, right, **kw):
    return lax.dot_general(left, right, (((1,), (1,)), ((), ())), preferred_element_type=F32, **kw)


def dot_nn(left, right, **kw):
    return lax.dot_general(left, right, (((1,), (0,)), ((), ())), preferred_element_type=F32, **kw)


def kernel(
    near_col, own_p, own_q, own_panel, target, near, sketch_t, near_out, far_out,
    buf_p, buf_q, buf_panel, total, left, sampled, grams,
    send_sem, recv_sem, panel_send, panel_recv, local_sem,
):
    place = Place()
    locals_ = [
        pltpu.make_async_copy(own_p, buf_p.at[:, 0], local_sem.at[0]),
        pltpu.make_async_copy(own_q, buf_q.at[:, 0], local_sem.at[1]),
        pltpu.make_async_copy(own_panel, buf_panel.at[0], local_sem.at[2]),
    ]
    for c in locals_:
        c.start()
    barrier = pltpu.get_barrier_semaphore()
    for axis, step in (("x", 1), ("x", -1), ("z", 1), ("z", -1), ("y", 1), ("y", -1), ("c", 1)):
        pl.semaphore_signal(barrier, inc=1, device_id=place.at(axis, step), device_id_type=MESH)
    pl.semaphore_wait(barrier, 7)
    for c in locals_:
        c.wait()

    sends = []
    counts = [0, 0]
    bufs = (buf_p, buf_q)

    def row_send(half, da, db, ring, step, parts):
        axis = ("xz" if half == 0 else "zx")[ring]
        src = row_slot(half, da, db)
        dst = row_slot(half, da - step, db) if ring == 0 else row_slot(half, da, db - step)
        for part in parts:
            c = pltpu.make_async_remote_copy(
                src_ref=bufs[part].at[half, src], dst_ref=bufs[part].at[half, dst],
                send_sem=send_sem.at[counts[0]], recv_sem=recv_sem.at[half, dst, part],
                device_id=place.at(axis, step), device_id_type=MESH,
            )
            counts[0] += 1
            c.start()
            sends.append(c)

    def row_wait(half, da, db):
        dst = row_slot(half, da, db)
        for part in (0, 1):
            ref = bufs[part].at[half, dst]
            pltpu.make_async_copy(ref, ref, recv_sem.at[half, dst, part]).wait()

    def panel_slot(dy, dc):
        return (dy % RING) * 2 + dc

    def panel_send_to(dy, dc, axis, step, parts):
        src = panel_slot(dy, dc)
        dst = panel_slot(dy - step, dc) if axis == "y" else panel_slot(dy, 1 - dc)
        for part in parts:
            c = pltpu.make_async_remote_copy(
                src_ref=buf_panel.at[src, part], dst_ref=buf_panel.at[dst, part],
                send_sem=panel_send.at[counts[1]], recv_sem=panel_recv.at[dst, part],
                device_id=place.at(axis, step), device_id_type=MESH,
            )
            counts[1] += 1
            c.start()
            sends.append(c)

    def panel_wait(dy, dc):
        dst = panel_slot(dy, dc)
        for part in (0, 1):
            ref = buf_panel.at[dst, part]
            pltpu.make_async_copy(ref, ref, panel_recv.at[dst, part]).wait()

    both = (0, 1)

    def onward(step):
        return (0,) if step == 1 else (1,)

    def start_blocks():
        lane = lax.broadcasted_iota(jnp.int32, (256, 128), 1)

        def body(n, carry):
            uv = target[n]
            v_only = jnp.where(lane >= 64, uv, jnp.zeros_like(uv))
            u_high = pltpu.roll(uv.astype(F32), 64, 1).astype(BF)
            is_near = near_col[n // 6] == lax.rem(n, 6)
            total[n] = dot_nt(v_only, u_high) * jnp.where(is_near, 0.0, 1.0)
            return carry

        lax.fori_loop(0, 24, body, 0)

    def group(half, slots):
        zeros = jnp.zeros((64, 256), BF)
        for g, slot in enumerate(slots):
            dx, dz = offsets(half, slot)
            xs, zs = lax.rem(place.x + dx, RING), lax.rem(place.z + dz, RING)
            dy = lax.rem(xs - place.y + RING, RING)
            dc = lax.rem(zs // 2 + place.core, 2)
            at = dy * 2 + dc
            first = lax.rem(zs, 2) * 2
            for kk in (0, 1):
                yhat = buf_panel[at, 0, first + kk]
                mid = dot_nn(buf_p[half, slot, kk, 0], yhat[:128]) + dot_nn(buf_p[half, slot, kk, 1], yhat[128:])
                mid = mid.astype(BF)
                for i in range(4):
                    xt = buf_panel[at, 1, first + kk, 64 * i : 64 * i + 64, :]
                    xt = jnp.concatenate([xt, zeros] if i % 2 == 0 else [zeros, xt], axis=0)
                    pair = mid[:, 128 * (i // 2) : 128 * (i // 2) + 128]
                    term = dot_nn(pair, xt).astype(BF)
                    for j in range(3):
                        left[i * 3 + j, g * 128 + kk * 64 : g * 128 + kk * 64 + 64, :] = term[64 * j : 64 * j + 64]

        def body(n, carry):
            j = lax.rem(n, 3)
            i = n // 3
            q = jnp.concatenate([buf_q[half, s, j] for s in slots], axis=1)
            at = i * 6 + half * 3 + j
            total[at] = total[at] - dot_nn(q, left[n, : 128 * len(slots)])
            return carry

        lax.fori_loop(0, 12, body, 0)

    for half in both:
        for step in (1, -1):
            row_send(half, 0, 0, 0, step, both)
    for step in (1, -1):
        panel_send_to(0, 0, "y", step, both)
    panel_send_to(0, 0, "c", 1, both)
    for half in both:
        for step in (1, -1):
            row_send(half, 0, 0, 1, step, both)
    start_blocks()
    for half in both:
        for step in (1, -1):
            row_wait(half, -step, 0)
            row_send(half, -step, 0, 0, step, onward(step))
            for step2 in (1, -1):
                row_send(half, -step, 0, 1, step2, both)
    for step in (1, -1):
        panel_wait(-step, 0)
        panel_send_to(-step, 0, "y", step, onward(step))
        panel_send_to(-step, 0, "c", 1, both)
    for half in both:
        for step in (1, -1):
            row_wait(half, 0, -step)
            row_send(half, 0, -step, 1, step, onward(step))
    for half in both:
        row_wait(half, 2, 0)
        for step in (1, -1):
            row_send(half, 2, 0, 1, step, both)
    panel_wait(2, 0)
    panel_send_to(2, 0, "c", 1, both)
    for dy in (0, 1, -1, 2):
        panel_wait(dy, 1)
    for half in both:
        group(half, [row_slot(half, *d) for d in ((0, 0), (1, 0), (-1, 0), (0, 1))])
    for da in (1, -1):
        for half in both:
            for step in (1, -1):
                row_wait(half, da, -step)
                row_send(half, da, -step, 1, step, onward(step))
    for half in both:
        group(half, [row_slot(half, *d) for d in ((0, -1), (2, 0), (1, 1), (1, -1))])
    for half in both:
        for step in (1, -1):
            row_wait(half, 2, -step)
            row_send(half, 2, -step, 1, step, onward(step))
    for half in both:
        group(half, [row_slot(half, *d) for d in ((-1, 1), (-1, -1), (2, 1), (2, -1))])
    for half in both:
        for da in (0, 1, -1, 2):
            row_wait(half, da, 2)
        group(half, [row_slot(half, *d) for d in ((0, 2), (1, 2), (-1, 2), (2, 2))])

    lane2 = lax.broadcasted_iota(jnp.int32, (64, 128), 1)
    sub2 = lax.broadcasted_iota(jnp.int32, (64, 128), 0)
    eye = jnp.where(lane2 == sub2, 1.0, 0.0).astype(F32)

    def sample(n, carry):
        z = dot_nn(sketch_t[lax.rem(n, 6)], total[n].astype(BF))
        sampled[n] = z
        z2 = jnp.concatenate([z, z], axis=0)
        gram = dot_nt(z, z2, precision=HIGH)
        grams[pl.ds(n, 64, stride=24), :] = jnp.where(lane2 >= 64, gram, eye)
        return carry

    lax.fori_loop(0, 24, sample, 0)

    lane24 = lax.broadcasted_iota(jnp.int32, (24, 128), 1)

    def eliminate(low):
        def body(j, carry):
            at = pl.ds(pl.multiple_of(j * 24, 8), 24)
            row = grams[at, :]
            pivot = jnp.sum(jnp.where(lane24 == 64 + j, row, 0.0), axis=1, keepdims=True)
            row = row * lax.rsqrt(pivot)
            grams[at, :] = row
            after = jnp.where(lane24 > 64 + j, row, 0.0)
            for c in range(low + 1, 64):
                grams[24 * c : 24 * c + 24, :] = grams[24 * c : 24 * c + 24, :] - after[:, 64 + c : 65 + c] * row
            return carry

        lax.fori_loop(low, low + 16, body, 0)

    for low in (0, 16, 32, 48):
        eliminate(low)

    def finish(n, carry):
        inverse = grams[pl.ds(n, 64, stride=24), :][:, :64]
        basis_t = (16.0 * dot_nn(inverse, sampled[n], precision=HIGH)).astype(BF)
        weight_t = (dot_nt(basis_t, total[n].astype(BF)) * (1.0 / 16.0)).astype(BF)
        is_near = near_col[n // 6] == lax.rem(n, 6)
        both_t = jnp.concatenate([basis_t, weight_t], axis=0).astype(F32)
        out = both_t.T
        far_out[n] = jnp.where(is_near, jnp.zeros_like(out), out).astype(BF)
        return carry

    lax.fori_loop(0, 24, finish, 0)

    def finish_near(i, carry):
        acc = total[i * 6]
        for j in range(1, 6):
            acc = jnp.where(near_col[i] == j, total[i * 6 + j], acc)
        near_out[i] = (near[i].astype(F32) + acc.T).astype(BF)
        return carry

    lax.fori_loop(0, 4, finish_near, 0)
    for c in sends:
        c.wait_send()


def prepare_rows(pivot_rows):
    p = pivot_rows[..., :64].reshape(2, 2, 3, 2, 128, 64)
    p = p.transpose(1, 0, 3, 2, 5, 4).reshape(2, 2, 2, 192, 128)
    q = pivot_rows[..., 64:].reshape(2, 2, 3, 256, 64)
    q = q.transpose(1, 2, 3, 0, 4).reshape(2, 3, 256, 128)
    return p, q


def prepare_panel(panel_cols, pivot_inv):
    yhat = jnp.einsum("kab,ikar->kbir", pivot_inv, panel_cols[..., 64:], preferred_element_type=F32)
    yhat = yhat.astype(BF).reshape(4, 256, 256)
    x_t = panel_cols[..., :64].transpose(1, 0, 3, 2).reshape(4, 256, 256)
    return jnp.stack([yhat, x_t])


def per_device(panel_cols, pivot_inv, pivot_rows, target_factors, near_blocks, near_cols, sketch):
    own_p, own_q = prepare_rows(pivot_rows)
    own_panel = prepare_panel(panel_cols, pivot_inv)
    sketch_t = sketch.transpose(0, 2, 1)
    any_ = pl.BlockSpec(memory_space=pl.ANY)
    vmem = pl.BlockSpec(memory_space=pltpu.VMEM)
    smem = pl.BlockSpec(memory_space=pltpu.SMEM)
    dma = pltpu.SemaphoreType.DMA
    near_new, far_new = pl.pallas_call(
        kernel,
        name="gather_and_eliminate",
        out_shape=(
            jax.ShapeDtypeStruct((4, 256, 256), BF),
            jax.ShapeDtypeStruct((24, 256, 128), BF),
        ),
        in_specs=[smem, any_, any_, any_, vmem, vmem, vmem],
        out_specs=(vmem, vmem),
        scratch_shapes=[
            pltpu.VMEM((2, 16, 2, 2, 192, 128), BF),
            pltpu.VMEM((2, 16, 3, 256, 128), BF),
            pltpu.VMEM((8, 2, 4, 256, 256), BF),
            pltpu.VMEM((24, 256, 256), F32),
            pltpu.VMEM((12, 512, 256), BF),
            pltpu.VMEM((24, 64, 256), F32),
            pltpu.VMEM((64 * 24, 128), F32),
            dma((60,)),
            dma((2, 16, 2)),
            dma((16,)),
            dma((8, 2)),
            dma((3,)),
        ],
        compiler_params=pltpu.CompilerParams(
            collective_id=0, has_side_effects=True, vmem_limit_bytes=56 << 20
        ),
    )(
        near_cols.reshape(4), own_p, own_q, own_panel,
        target_factors.reshape(24, 256, 128), near_blocks.reshape(4, 256, 256), sketch_t,
    )
    return near_new.reshape(near_blocks.shape), far_new.reshape(target_factors.shape)


def solution(mesh):
    placed = (
        P("rows", "cols", None, None),
        P("cols", None, None),
        P("rows", "cols", None, None),
        P("rows", "cols", None, None),
        P("rows", "cols", None, None),
        P("rows", "cols"),
        P("cols", None, None),
    )
    return jax.shard_map(
        per_device,
        mesh=mesh,
        in_specs=placed,
        out_specs=(P("rows", "cols", None, None), P("rows", "cols", None, None)),
        check_vma=False,
    )
```

time: 2010 us -> 151 us (0.08)
  waiting for transfers between devices: 1430 us -> 0 us
  other arithmetic: 278 us -> 1.06 us
  local copies, waits for them, and re-layouts: 151 us -> 9.51 us
  Pallas kernels: 0 us -> 139 us
  matrix products: 118 us -> 0.48 us
    psum x16 -> x0, waiting for transfers between devices: 1430 us -> none  [spread(): return lax.psum(block, axis)]
    another operation x28 -> x1, other arithmetic: 260 us -> 1.06 us  [prepare_panel(): return jnp.stack([yhat, x_t])]
    pallas_call x0 -> x1, Pallas kernels: none -> 139 us  [per_device(): pl.pallas_call(kernel, name='gather_and_eliminate', out_shape=(jax.ShapeD...]
    dot_general x30 -> x1, matrix products: 116 us -> 0.48 us  [prepare_panel(): jnp.einsum('kab,ikar->kbir', pivot_inv, panel_cols[..., 64:], preferred_e...]
    while x3 -> x0, local copies, waits for them, and re-layouts: 38.1 us -> none  [the longest x2 21.3 us: per_device(): lax.map(one_row, (panel_all, target_factors, near_blocks, near_cols))]
    dynamic_update_slice x24 -> x0, local copies, waits for them, and re-layouts: 37.3 us -> none  [the longest x16 33.3 us: fetch(): lax.dynamic_update_slice_in_dim(buffer, arrived, (owner * owned).astype(j...]
    dynamic_slice x20 -> x0, local copies, waits for them, and re-layouts: 32.8 us -> none  [per_device(): lax.map(one_row, (panel_all, target_factors, near_blocks, near_cols))]
    another operation x4 -> x1, local copies, waits for them, and re-layouts: 25 us -> 0.2 us  [prepare_panel(): return jnp.stack([yhat, x_t])]
  transfers between devices with their start and end apart: 17 -> 0, of which waited for: 17 -> 0; matrix products, arithmetic and copies ran while one was open for 2% -> 0% of each run, Pallas kernels for 0% -> 0%
where the time goes in v1:
time: 151 us
  Pallas kernels  139 us (92%)
  local copies, waits for them, and re-layouts  9.51 us (6%)
    pallas_call x1, Pallas kernels, per_device(): pl.pallas_call(kernel, name='gather_and_eliminate', out_shape=(jax.ShapeD...  139 us
    unnamed x6, local copies, waits for them, and re-layouts  4.59 us

profile of v1, /device:TPU:1, one launch (start us, length us, event | category | flops | bytes accessed | tf_op | source)
XLA Modules:
  0.0 150.8 jit_solution(10369908895604204481)
XLA Ops:
  0.6 0.0 copy-start
  0.6 1.8 %fusion.3 = (bf16[2,6,256,64]{3,2,1,0:T(8,128)(2,1)S(1)}, bf16[2,6,256,64]{3,2,1,0:T(8,128)(2,1)S(1)}) fusion(bf16[2,6,256,128]{3,2,1,0:T(8,128)(2,1)} %param.9), kind=kLoop, calls=%fused_computation.6 | loop fusion | bytes 1572864 | tf_op jit(solution)/shard_map/slice | solution.py:275
  2.4 0.0 copy-start.1
  2.4 0.3 copy.16
  2.7 0.9 copy.20.own_q
  3.6 1.0 copy.15
  4.6 0.0 copy-done.1
  4.6 0.4 fusion.2
  5.1 0.0 copy-done
  5.1 0.5 convolution_convert_fusion
  5.6 0.2 copy.19
  5.8 0.3 copy.18
  6.1 1.1 pad_maximum_fusion.own_panel
  7.2 139.1 %gather_and_eliminate.1 = (bf16[4,256,256]{2,1,0:T(8,128)(2,1)}, bf16[24,256,128]{2,1,0:T(8,128)(2,1)}) custom-call(s32[4]{0:T(128)} %bitcast.36, bf16[2,2,2,192,128]{4,3,2,1,0:T(8,128)(2,1)} %bitcast.31, bf16[2,3,256,128]{3,2,1,0:T(8,128)(2,1)} %copy.20.own_q, bf16[2,4,256,256]{3,2,1,0:T(8,128)(2,1)} %pad_maximum_fusion.own_panel, ...), custom_call_target="tpu_custom_call" | custom-call | tf_op jit(solution)/shard_map/gather_and_eliminate/pallas_call | solution.py:295
  146.3 1.9 %copy.28 = bf16[4,1,256,256]{3,2,1,0:T(8,128)(2,1)} copy(bf16[4,1,256,256]{3,2,1,0:T(8,128)(2,1)} %bitcast.34) | data formatting | bytes 1048576
  148.1 2.7 %copy.29 = bf16[4,6,256,128]{3,2,1,0:T(8,128)(2,1)} copy(bf16[4,6,256,128]{3,2,1,0:T(8,128)(2,1)} %bitcast.30) | data formatting | bytes 3145728
Async XLA Ops:
  0.6 4.4 %copy-start = (bf16[4,256,256]{2,1,0:T(8,128)(2,1)S(1)}, bf16[4,256,256]{2,1,0:T(8,128)(2,1)}, u32[]{:S(2)}) copy-start(bf16[4,256,256]{2,1,0:T(8,128)(2,1)} %param.8) | copy-start | bytes 1572868
  2.4 2.2 %copy-start.1 = (bf16[4,4,256,128]{3,2,1,0:T(8,128)(2,1)S(1)}, bf16[4,4,256,128]{3,2,1,0:T(8,128)(2,1)}, u32[]{:S(2)}) copy-start(bf16[4,4,256,128]{3,2,1,0:T(8,128)(2,1)} %param.7) | copy-start | bytes 3145732

commit v2 on v1

v2 whole, which is shorter than its diff:
```python
import jax
import jax.numpy as jnp
from jax import lax
from jax.experimental import pallas as pl
from jax.experimental.pallas import tpu as pltpu
from jax.sharding import PartitionSpec as P

MESH = pl.DeviceIdType.MESH
BF = jnp.bfloat16
F32 = jnp.float32
HIGH = lax.Precision.HIGHEST
RING = 4
PANEL = 16


class Place:
    def __init__(self):
        self.row, self.col = lax.axis_index("rows"), lax.axis_index("cols")
        self.x, self.z = self.row // RING, self.row % RING
        self.y, self.core = self.col // 2, self.col % 2

    def at(self, axis, step):
        if axis == "x":
            return (lax.rem(self.x + step + RING, RING) * RING + self.z, self.col)
        if axis == "z":
            return (self.x * RING + lax.rem(self.z + step + RING, RING), self.col)
        if axis == "y":
            return (self.row, lax.rem(self.y + step + RING, RING) * 2 + self.core)
        return (self.row, self.y * 2 + (1 - self.core))


def row_slot(half, da, db):
    dx, dz = (da, db) if half == 0 else (db, da)
    return (dx % RING) * RING + dz % RING


def offsets(half, slot):
    return slot // RING, slot % RING


def dot_nt(left, right, **kw):
    return lax.dot_general(left, right, (((1,), (1,)), ((), ())), preferred_element_type=F32, **kw)


def dot_nn(left, right, **kw):
    return lax.dot_general(left, right, (((1,), (0,)), ((), ())), preferred_element_type=F32, **kw)


def kernel(
    near_col, rows_hbm, panel_hbm, inv_hbm, target_hbm, near_hbm, sketch_hbm, near_out, far_out,
    raw_rows, raw_panel, raw_inv, target, near, sketch_t, near_new, far_new,
    buf_p, buf_q, buf_panel, total, left, sampled, grams,
    send_sem, recv_sem, panel_send, panel_recv, local_sem, out_sem,
):
    place = Place()
    loads = [
        pltpu.make_async_copy(src, dst, local_sem.at[i])
        for i, (src, dst) in enumerate(
            (
                (rows_hbm, raw_rows), (panel_hbm, raw_panel), (inv_hbm, raw_inv),
                (target_hbm, target), (sketch_hbm, sketch_t), (near_hbm, near),
            )
        )
    ]
    for c in loads:
        c.start()
    barrier = pltpu.get_barrier_semaphore()
    for axis, step in (("x", 1), ("x", -1), ("z", 1), ("z", -1), ("y", 1), ("y", -1), ("c", 1)):
        pl.semaphore_signal(barrier, inc=1, device_id=place.at(axis, step), device_id_type=MESH)

    loads[0].wait()
    for j in range(6):
        half, jj = j // 3, j % 3
        for kk in (0, 1):
            buf_p[half, 0, kk, 64 * jj : 64 * jj + 64, :] = raw_rows[kk, j].T[:64]
        buf_q[half, 0, jj] = jnp.concatenate([raw_rows[0, j][:, 64:], raw_rows[1, j][:, 64:]], axis=1)
    pl.semaphore_wait(barrier, 7)

    sends = []
    counts = [0, 0]
    bufs = (buf_p, buf_q)

    def row_send(half, da, db, ring, step, part):
        axis = ("xz" if half == 0 else "zx")[ring]
        src = row_slot(half, da, db)
        dst = row_slot(half, da - step, db) if ring == 0 else row_slot(half, da, db - step)
        c = pltpu.make_async_remote_copy(
            src_ref=bufs[part].at[half, src], dst_ref=bufs[part].at[half, dst],
            send_sem=send_sem.at[counts[0]], recv_sem=recv_sem.at[half, dst, part],
            device_id=place.at(axis, step), device_id_type=MESH,
        )
        counts[0] += 1
        c.start()
        sends.append(c)

    def row_wait(half, da, db, part):
        dst = row_slot(half, da, db)
        ref = bufs[part].at[half, dst]
        pltpu.make_async_copy(ref, ref, recv_sem.at[half, dst, part]).wait()

    def panel_slot(dy, dc):
        return (dy % RING) * 2 + dc

    def panel_send_to(dy, dc, axis, step, part):
        src = panel_slot(dy, dc)
        dst = panel_slot(dy - step, dc) if axis == "y" else panel_slot(dy, 1 - dc)
        c = pltpu.make_async_remote_copy(
            src_ref=buf_panel.at[src, part], dst_ref=buf_panel.at[dst, part],
            send_sem=panel_send.at[counts[1]], recv_sem=panel_recv.at[dst, part],
            device_id=place.at(axis, step), device_id_type=MESH,
        )
        counts[1] += 1
        c.start()
        sends.append(c)

    def panel_wait(dy, dc, part):
        dst = panel_slot(dy, dc)
        ref = buf_panel.at[dst, part]
        pltpu.make_async_copy(ref, ref, panel_recv.at[dst, part]).wait()

    both = (0, 1)

    def onward(step):
        return 0 if step == 1 else 1

    def prepare_panel():
        for k in range(4):
            turned = [raw_panel[i, k].T for i in range(4)]
            for i in range(4):
                buf_panel[0, k, 1, 64 * i : 64 * i + 64, :] = turned[i][:64]
            y_t = jnp.concatenate([t[64:] for t in turned], axis=0)
            buf_panel[0, k, 0] = dot_nn(y_t, raw_inv[k]).astype(BF)

    def start_blocks():
        lane = lax.broadcasted_iota(jnp.int32, (256, 128), 1)

        def body(n, carry):
            uv = target[n]
            v_only = jnp.where(lane >= 64, uv, jnp.zeros_like(uv))
            u_high = pltpu.roll(uv.astype(F32), 64, 1).astype(BF)
            is_near = near_col[n // 6] == lax.rem(n, 6)
            total[n] = dot_nt(v_only, u_high) * jnp.where(is_near, 0.0, 1.0)
            return carry

        lax.fori_loop(0, 24, body, 0)

    def group(half, places):
        slots = [row_slot(half, *d) for d in places]
        zeros = jnp.zeros((64, 256), BF)
        todo = []
        for g, slot in enumerate(slots):
            dx, dz = offsets(half, slot)
            xs, zs = lax.rem(place.x + dx, RING), lax.rem(place.z + dz, RING)
            dy = lax.rem(xs - place.y + RING, RING)
            dc = lax.rem(zs // 2 + place.core, 2)
            at = dy * 2 + dc
            for kk in (0, 1):
                k = lax.rem(zs, 2) * 2 + kk
                mid = dot_nt(buf_p[half, slot, kk], buf_panel[at, k, 0]).astype(BF)
                todo.append((mid, at, k, g * 128 + kk * 64))
        for mid, at, k, low in todo:
            for i in range(4):
                xt = buf_panel[at, k, 1, 64 * i : 64 * i + 64, :]
                xt = jnp.concatenate([xt, zeros] if i % 2 == 0 else [zeros, xt], axis=0)
                pair = mid[:, 128 * (i // 2) : 128 * (i // 2) + 128]
                term = dot_nn(pair, xt).astype(BF)
                for j in range(3):
                    left[i * 3 + j, low : low + 64, :] = term[64 * j : 64 * j + 64]
        for j in range(3):
            q = jnp.concatenate([buf_q[half, s, j] for s in slots], axis=1)
            for i in range(4):
                at = i * 6 + half * 3 + j
                total[at] = total[at] - dot_nn(q, left[i * 3 + j, : 128 * len(slots)])

    for part in both:
        for half in both:
            for step in (1, -1):
                row_send(half, 0, 0, 0, step, part if step == 1 else 1 - part)
    loads[1].wait()
    loads[2].wait()
    prepare_panel()
    for k in range(4):
        for step in (1, -1):
            panel_send_to(0, 0, "y", step, k if step == 1 else (k + 2) % 4)
    for k in range(4):
        panel_send_to(0, 0, "c", 1, k)
    for part in both:
        for half in both:
            for step in (1, -1):
                row_send(half, 0, 0, 1, step, part if step == 1 else 1 - part)
    loads[3].wait()
    start_blocks()
    for first in (True, False):
        for half in both:
            for step in (1, -1):
                part = onward(step) if first else 1 - onward(step)
                row_wait(half, -step, 0, part)
                if first:
                    row_send(half, -step, 0, 0, step, part)
                for step2 in (1, -1):
                    row_send(half, -step, 0, 1, step2, part)
    for k in range(4):
        for step in (1, -1):
            part = k if step == 1 else (k + 2) % 4
            panel_wait(-step, 0, part)
            if k < 2:
                panel_send_to(-step, 0, "y", step, part)
            panel_send_to(-step, 0, "c", 1, part)

    def turn(half, da):
        for first in (True, False):
            for step in (1, -1):
                part = onward(step) if first else 1 - onward(step)
                row_wait(half, da, -step, part)
                if first:
                    row_send(half, da, -step, 1, step, part)

    for half in both:
        turn(half, 0)
    for half in both:
        for part in both:
            row_wait(half, 2, 0, part)
            for step in (1, -1):
                row_send(half, 2, 0, 1, step, part)
    for part in (0, 2, 1, 3):
        panel_wait(2, 0, part)
        panel_send_to(2, 0, "c", 1, part)
    for dy in (0, 1, -1, 2):
        for part in range(4):
            panel_wait(dy, 1, part)

    def last(half, das):
        for da in das:
            for part in both:
                row_wait(half, da, 2, part)

    group(0, ((0, 0), (1, 0), (-1, 0), (0, 1)))
    for half in both:
        turn(half, 1)
        turn(half, -1)
    group(1, ((0, 0), (1, 0), (-1, 0), (0, 1)))
    for half in both:
        turn(half, 2)
    for half in both:
        group(half, ((0, -1), (2, 0), (1, 1), (1, -1)))
    for half in both:
        group(half, ((-1, 1), (-1, -1), (2, 1), (2, -1)))
    for half in both:
        last(half, (0, 1))
        group(half, ((0, 2), (1, 2)))
    for half in both:
        last(half, (-1, 2))
        group(half, ((-1, 2), (2, 2)))

    for c in loads[4:]:
        c.wait()
    lane2 = lax.broadcasted_iota(jnp.int32, (64, 128), 1)
    sub2 = lax.broadcasted_iota(jnp.int32, (64, 128), 0)
    eye = jnp.where(lane2 == sub2, 1.0, 0.0).astype(F32)

    stores = []
    for i in range(4):
        acc = total[i * 6]
        for j in range(1, 6):
            acc = jnp.where(near_col[i] == j, total[i * 6 + j], acc)
        near_new[i] = (near[i].astype(F32) + acc.T).astype(BF)
    stores.append(pltpu.make_async_copy(near_new, near_out, out_sem.at[0]))
    stores[-1].start()

    for n in range(24):
        z = dot_nn(sketch_t[n % 6], total[n].astype(BF))
        sampled[n] = z
        z2 = jnp.concatenate([z, z], axis=0)
        gram = dot_nt(z, z2, precision=HIGH)
        grams[pl.ds(n, 64, stride=24), :] = jnp.where(lane2 >= 64, gram, eye)

    for base in range(0, 64, PANEL):
        rows = [grams[24 * c : 24 * c + 24, :] for c in range(base, base + PANEL)]
        for t in range(PANEL):
            row = rows[t]
            pivot = row[:, 64 + base + t : 65 + base + t]
            scaled = row * (1.0 / pivot)
            for u in range(t + 1, PANEL):
                rows[u] = rows[u] - row[:, 64 + base + u : 65 + base + u] * scaled
            rows[t] = row * lax.rsqrt(pivot)
            grams[24 * (base + t) : 24 * (base + t) + 24, :] = rows[t]
        after = base + PANEL
        if after < 64:
            for n in range(24):
                done = grams[pl.ds(24 * base + n, PANEL, stride=24), :]
                rest = pl.ds(24 * after + n, 64 - after, stride=24)
                grams[rest, :] = grams[rest, :] - dot_nn(done.T[64 + after :], done, precision=HIGH)

    for n in range(24):
        inverse = grams[pl.ds(n, 64, stride=24), :][:, :64]
        basis_t = (16.0 * dot_nn(inverse, sampled[n], precision=HIGH)).astype(BF)
        weight_t = (dot_nt(basis_t, total[n].astype(BF)) * (1.0 / 16.0)).astype(BF)
        out = jnp.concatenate([basis_t, weight_t], axis=0).T
        far_new[n] = jnp.where(near_col[n // 6] == n % 6, jnp.zeros_like(out), out)
        if n % 6 == 5:
            done = pl.ds(n - 5, 6)
            stores.append(pltpu.make_async_copy(far_new.at[done], far_out.at[done], out_sem.at[1 + n // 6]))
            stores[-1].start()

    for c in sends:
        c.wait_send()
    for c in stores:
        c.wait()


def per_device(panel_cols, pivot_inv, pivot_rows, target_factors, near_blocks, near_cols, sketch):
    any_ = pl.BlockSpec(memory_space=pl.ANY)
    smem = pl.BlockSpec(memory_space=pltpu.SMEM)
    dma = pltpu.SemaphoreType.DMA
    near_new, far_new = pl.pallas_call(
        kernel,
        name="gather_and_eliminate",
        out_shape=(
            jax.ShapeDtypeStruct((4, 256, 256), BF),
            jax.ShapeDtypeStruct((24, 256, 128), BF),
        ),
        in_specs=[smem] + [any_] * 6,
        out_specs=(any_, any_),
        scratch_shapes=[
            pltpu.VMEM((2, 6, 256, 128), BF),
            pltpu.VMEM((4, 4, 256, 128), BF),
            pltpu.VMEM((4, 256, 256), BF),
            pltpu.VMEM((24, 256, 128), BF),
            pltpu.VMEM((4, 256, 256), BF),
            pltpu.VMEM((6, 64, 256), BF),
            pltpu.VMEM((4, 256, 256), BF),
            pltpu.VMEM((24, 256, 128), BF),
            pltpu.VMEM((2, 16, 2, 192, 256), BF),
            pltpu.VMEM((2, 16, 3, 256, 128), BF),
            pltpu.VMEM((8, 4, 2, 256, 256), BF),
            pltpu.VMEM((24, 256, 256), F32),
            pltpu.VMEM((12, 512, 256), BF),
            pltpu.VMEM((24, 64, 256), F32),
            pltpu.VMEM((64 * 24, 128), F32),
            dma((60,)),
            dma((2, 16, 2)),
            dma((28,)),
            dma((8, 4)),
            dma((6,)),
            dma((5,)),
        ],
        compiler_params=pltpu.CompilerParams(
            collective_id=0, has_side_effects=True, vmem_limit_bytes=56 << 20
        ),
    )(
        near_cols.reshape(4), pivot_rows, panel_cols, pivot_inv,
        target_factors.reshape(24, 256, 128), near_blocks.reshape(4, 256, 256), sketch.transpose(0, 2, 1),
    )
    return near_new.reshape(near_blocks.shape), far_new.reshape(target_factors.shape)


def solution(mesh):
    placed = (
        P("rows", "cols", None, None),
        P("cols", None, None),
        P("rows", "cols", None, None),
        P("rows", "cols", None, None),
        P("rows", "cols", None, None),
        P("rows", "cols"),
        P("cols", None, None),
    )
    return jax.shard_map(
        per_device,
        mesh=mesh,
        in_specs=placed,
        out_specs=(P("rows", "cols", None, None), P("rows", "cols", None, None)),
        check_vma=False,
    )
```

time: 151 us -> 100 us (0.66)
  Pallas kernels: 139 us -> 94.5 us
  local copies, waits for them, and re-layouts: 9.51 us -> 4.57 us
    pallas_call x1, Pallas kernels: 139 us -> 94.5 us  [per_device(): pl.pallas_call(kernel, name='gather_and_eliminate', out_shape=(jax.ShapeD...]
    slice x3 -> x0, local copies, waits for them, and re-layouts: 2.47 us -> none  [the longest x2 2.02 us: prepare_rows(): q = pivot_rows[..., 64:].reshape(2, 2, 3, 256, 64)]
    reshape x2 -> x0, local copies, waits for them, and re-layouts: 1.92 us -> none  [the longest x1 1.01 us: prepare_rows(): p = pivot_rows[..., :64].reshape(2, 2, 3, 2, 128, 64)]
    unnamed x6 -> x2, local copies, waits for them, and re-layouts: 4.59 us -> 4.57 us
where the time goes in v2:
time: 100 us; the launch traced here: 99.7 us
  Pallas kernels  94.5 us (94%)
  local copies, waits for them, and re-layouts  4.57 us (5%)
    pallas_call x1, Pallas kernels, per_device(): pl.pallas_call(kernel, name='gather_and_eliminate', out_shape=(jax.ShapeD...  94.5 us
    unnamed x2, local copies, waits for them, and re-layouts  4.57 us

profile of v2, /device:TPU:1, one launch (start us, length us, event | category | flops | bytes accessed | tf_op | source)
XLA Modules:
  0.0 99.7 jit_solution(17837413285180527814)
XLA Ops:
  0.6 94.5 %gather_and_eliminate.1 = (bf16[4,256,256]{2,1,0:T(8,128)(2,1)}, bf16[24,256,128]{2,1,0:T(8,128)(2,1)}) custom-call(s32[4]{0:T(128)} %bitcast.13, bf16[2,6,256,128]{3,2,1,0:T(8,128)(2,1)} %rows_hbm.1, bf16[4,4,256,128]{3,2,1,0:T(8,128)(2,1)} %panel_hbm.1, bf16[4,256,256]{2,1,0:T(8,128)(2,1)} %inv_hbm.1, bf16[24,256,128]{2,1,0:T(8,128)(2,1)} %bitcast.9, ...), custom_call_target="tpu_custom_call" | custom-call | tf_op jit(solution)/shard_map/gather_and_eliminate/pallas_call | solution.py:315
  95.1 1.9 %copy.12 = bf16[4,1,256,256]{3,2,1,0:T(8,128)(2,1)} copy(bf16[4,1,256,256]{3,2,1,0:T(8,128)(2,1)} %bitcast.11) | data formatting | bytes 1048576
  97.0 2.7 %copy.13 = bf16[4,6,256,128]{3,2,1,0:T(8,128)(2,1)} copy(bf16[4,6,256,128]{3,2,1,0:T(8,128)(2,1)} %bitcast.8) | data formatting | bytes 3145728

commit v3 on v2

--- a/solution.py
+++ b/solution.py
@@ -11,6 +11,16 @@
 HIGH = lax.Precision.HIGHEST
 RING = 4
 PANEL = 16
+
+
+def dot_split(left, right):
+    left_high, right_high = left.astype(BF), right.astype(BF)
+    left_low = (left - left_high.astype(F32)).astype(BF)
+    right_low = (right - right_high.astype(F32)).astype(BF)
+    return dot_nn(
+        jnp.concatenate([left_high, left_low, left_high], axis=1),
+        jnp.concatenate([right_high, right_high, right_low], axis=0),
+    )
 
 
 class Place:
@@ -128,7 +138,7 @@
             turned = [raw_panel[i, k].T for i in range(4)]
             for i in range(4):
                 buf_panel[0, k, 1, 64 * i : 64 * i + 64, :] = turned[i][:64]
-            y_t = jnp.concatenate([t[64:] for t in turned], axis=0)
+            y_t = jnp.concatenate([turned[i ^ (k % 2)][64:] for i in range(4)], axis=0)
             buf_panel[0, k, 0] = dot_nn(y_t, raw_inv[k]).astype(BF)
 
     def start_blocks():
@@ -146,26 +156,34 @@
 
     def group(half, places):
         slots = [row_slot(half, *d) for d in places]
-        zeros = jnp.zeros((64, 256), BF)
+        low = lax.broadcasted_iota(jnp.int32, (192, 128), 1) < 64
         todo = []
-        for g, slot in enumerate(slots):
+        for slot in slots:
             dx, dz = offsets(half, slot)
             xs, zs = lax.rem(place.x + dx, RING), lax.rem(place.z + dz, RING)
             dy = lax.rem(xs - place.y + RING, RING)
             dc = lax.rem(zs // 2 + place.core, 2)
             at = dy * 2 + dc
-            for kk in (0, 1):
-                k = lax.rem(zs, 2) * 2 + kk
-                mid = dot_nt(buf_p[half, slot, kk], buf_panel[at, k, 0]).astype(BF)
-                todo.append((mid, at, k, g * 128 + kk * 64))
-        for mid, at, k, low in todo:
-            for i in range(4):
-                xt = buf_panel[at, k, 1, 64 * i : 64 * i + 64, :]
-                xt = jnp.concatenate([xt, zeros] if i % 2 == 0 else [zeros, xt], axis=0)
-                pair = mid[:, 128 * (i // 2) : 128 * (i // 2) + 128]
-                term = dot_nn(pair, xt).astype(BF)
-                for j in range(3):
-                    left[i * 3 + j, low : low + 64, :] = term[64 * j : 64 * j + 64]
+            k = lax.rem(zs, 2) * 2
+            mids = [dot_nt(buf_p[half, slot, kk], buf_panel[at, k + kk, 0]).astype(BF) for kk in (0, 1)]
+            todo.append((mids, at, k))
+        for g, (mids, at, k) in enumerate(todo):
+            for q in (0, 1):
+                one, two = (m[:, 128 * q : 128 * q + 128] for m in mids)
+                none = jnp.zeros_like(one)
+                for i in (2 * q, 2 * q + 1):
+                    x_one, x_two = (buf_panel[at, k + kk, 1, 64 * i : 64 * i + 64, :] for kk in (0, 1))
+                    if i % 2 == 0:
+                        mid = jnp.concatenate([jnp.where(low, one, none), jnp.where(low, none, two)], axis=0)
+                        x_t = jnp.concatenate([x_one, x_two], axis=0)
+                    else:
+                        mid = jnp.concatenate([jnp.where(low, none, one), jnp.where(low, two, none)], axis=0)
+                        x_t = jnp.concatenate([x_two, x_one], axis=0)
+                    term = dot_nn(mid, x_t).astype(BF)
+                    for kk in (0, 1):
+                        for j in range(3):
+                            at_row = 192 * kk + 64 * j
+                            left[i * 3 + j, g * 128 + kk * 64 : g * 128 + kk * 64 + 64, :] = term[at_row : at_row + 64]
         for j in range(3):
             q = jnp.concatenate([buf_q[half, s, j] for s in slots], axis=1)
             for i in range(4):
@@ -246,11 +264,11 @@
     for half in both:
         group(half, ((-1, 1), (-1, -1), (2, 1), (2, -1)))
     for half in both:
-        last(half, (0, 1))
-        group(half, ((0, 2), (1, 2)))
-    for half in both:
-        last(half, (-1, 2))
-        group(half, ((-1, 2), (2, 2)))
+        last(half, (0, 1, -1))
+        group(half, ((0, 2), (1, 2), (-1, 2)))
+    for half in both:
+        last(half, (2,))
+        group(half, ((2, 2),))
 
     for c in loads[4:]:
         c.wait()
@@ -276,14 +294,27 @@
 
     for base in range(0, 64, PANEL):
         rows = [grams[24 * c : 24 * c + 24, :] for c in range(base, base + PANEL)]
-        for t in range(PANEL):
-            row = rows[t]
-            pivot = row[:, 64 + base + t : 65 + base + t]
-            scaled = row * (1.0 / pivot)
-            for u in range(t + 1, PANEL):
-                rows[u] = rows[u] - row[:, 64 + base + u : 65 + base + u] * scaled
-            rows[t] = row * lax.rsqrt(pivot)
-            grams[24 * (base + t) : 24 * (base + t) + 24, :] = rows[t]
+        for low in range(0, PANEL, 4):
+
+            def entry(t, c):
+                at = 64 + base + low + c
+                return jnp.broadcast_to(rows[low + t][:, at : at + 1], (24, 128))
+
+            corner = {(t, c): entry(t, c) for t in range(4) for c in range(t, 4)}
+            for t in range(4):
+                row = rows[low + t]
+                inverse = 1.0 / corner[t, t]
+                scaled = row * inverse
+                for u in range(t + 1, 4):
+                    rows[low + u] = rows[low + u] - corner[t, u] * scaled
+                    factor = corner[t, u] * inverse
+                    for c in range(u, 4):
+                        corner[u, c] = corner[u, c] - factor * corner[t, c]
+                for u in range(low + 4, PANEL):
+                    rows[u] = rows[u] - row[:, 64 + base + u : 65 + base + u] * scaled
+                rows[low + t] = row * lax.rsqrt(corner[t, t])
+                at = 24 * (base + low + t)
+                grams[at : at + 24, :] = rows[low + t]
         after = base + PANEL
         if after < 64:
             for n in range(24):
@@ -293,7 +324,7 @@
 
     for n in range(24):
         inverse = grams[pl.ds(n, 64, stride=24), :][:, :64]
-        basis_t = (16.0 * dot_nn(inverse, sampled[n], precision=HIGH)).astype(BF)
+        basis_t = (16.0 * dot_split(inverse, sampled[n])).astype(BF)
         weight_t = (dot_nt(basis_t, total[n].astype(BF)) * (1.0 / 16.0)).astype(BF)
         out = jnp.concatenate([basis_t, weight_t], axis=0).T
         far_new[n] = jnp.where(near_col[n // 6] == n % 6, jnp.zeros_like(out), out)
@@ -304,6 +335,21 @@
 
     for c in sends:
         c.wait_send()
+    for c in stores:
+        c.wait()
+
+
+def hand_over(near_new, far_new, near_out, far_out, near, far, sem):
+    whole = pl.ds(0, 4)
+    pieces = [(near_new, near, near_out, whole)]
+    pieces += [(far_new, far, far_out, pl.ds(4 * n, 4)) for n in range(6)]
+    loads = [pltpu.make_async_copy(src.at[at], mid.at[at], sem.at[0, n]) for n, (src, mid, _, at) in enumerate(pieces)]
+    stores = [pltpu.make_async_copy(mid.at[at], dst.at[at], sem.at[1, n]) for n, (_, mid, dst, at) in enumerate(pieces)]
+    for c in loads:
+        c.start()
+    for load, store in zip(loads, stores):
+        load.wait()
+        store.start()
     for c in stores:
         c.wait()
 
@@ -351,6 +397,17 @@
         near_cols.reshape(4), pivot_rows, panel_cols, pivot_inv,
         target_factors.reshape(24, 256, 128), near_blocks.reshape(4, 256, 256), sketch.transpose(0, 2, 1),
     )
+    near_new, far_new = pl.pallas_call(
+        hand_over,
+        name="hand_over",
+        out_shape=(
+            jax.ShapeDtypeStruct(near_new.shape, BF),
+            jax.ShapeDtypeStruct(far_new.shape, BF),
+        ),
+        in_specs=[any_, any_],
+        out_specs=(any_, any_),
+        scratch_shapes=[pltpu.VMEM((4, 256, 256), BF), pltpu.VMEM((24, 256, 128), BF), dma((2, 7))],
+    )(near_new, far_new)
     return near_new.reshape(near_blocks.shape), far_new.reshape(target_factors.shape)
 
 

time: 100 us -> 92.5 us (0.925)
  local copies, waits for them, and re-layouts: 4.57 us -> 0 us
  Pallas kernels: 94.5 us -> 90.6 us
    pallas_call x1, Pallas kernels: 94.5 us -> 88.1 us  [per_device(): pl.pallas_call(kernel, name='gather_and_eliminate', out_shape=(jax.ShapeD...]
    unnamed x2 -> x0, local copies, waits for them, and re-layouts: 4.57 us -> none
    pallas_call x0 -> x1, Pallas kernels: none -> 2.47 us  [per_device(): pl.pallas_call(hand_over, name='hand_over', out_shape=(jax.ShapeDtypeStru...]
where the time goes in v3:
time: 92.5 us; the launch traced here: 91.4 us
  Pallas kernels  90.6 us (98%)
    pallas_call x1, Pallas kernels, per_device(): pl.pallas_call(kernel, name='gather_and_eliminate', out_shape=(jax.ShapeD...  88.1 us
    pallas_call x1, Pallas kernels, per_device(): pl.pallas_call(hand_over, name='hand_over', out_shape=(jax.ShapeDtypeStru...  2.47 us

profile of v3, /device:TPU:1, one launch (start us, length us, event | category | flops | bytes accessed | tf_op | source)
XLA Modules:
  0.0 91.4 jit_solution(13596442271588478363)
XLA Ops:
  0.6 88.1 %gather_and_eliminate.1 = (bf16[4,256,256]{2,1,0:T(8,128)(2,1)}, bf16[24,256,128]{2,1,0:T(8,128)(2,1)}) custom-call(s32[4]{0:T(128)} %bitcast.11, bf16[2,6,256,128]{3,2,1,0:T(8,128)(2,1)} %rows_hbm.1, bf16[4,4,256,128]{3,2,1,0:T(8,128)(2,1)} %panel_hbm.1, bf16[4,256,256]{2,1,0:T(8,128)(2,1)} %inv_hbm.1, bf16[24,256,128]{2,1,0:T(8,128)(2,1)} %bitcast.8, ...), custom_call_target="tpu_custom_call" | custom-call | tf_op jit(solution)/shard_map/gather_and_eliminate/pallas_call | solution.py:361
  88.8 2.5 %hand_over.1 = (bf16[4,256,256]{2,1,0:T(8,128)(2,1)}, bf16[24,256,128]{2,1,0:T(8,128)(2,1)}) custom-call(bf16[4,256,256]{2,1,0:T(8,128)(2,1)} %get-tuple-element.6.near_new, bf16[24,256,128]{2,1,0:T(8,128)(2,1)} %get-tuple-element.7.far_new), custom_call_target="tpu_custom_call" | custom-call | tf_op jit(solution)/shard_map/hand_over/pallas_call | solution.py:400

commit v4 on v3

--- a/solution.py
+++ b/solution.py
@@ -72,13 +72,14 @@
             )
         )
     ]
-    for c in loads:
-        c.start()
+    loads[0].start()
     barrier = pltpu.get_barrier_semaphore()
     for axis, step in (("x", 1), ("x", -1), ("z", 1), ("z", -1), ("y", 1), ("y", -1), ("c", 1)):
         pl.semaphore_signal(barrier, inc=1, device_id=place.at(axis, step), device_id_type=MESH)
 
     loads[0].wait()
+    for c in loads[1:]:
+        c.start()
     for j in range(6):
         half, jj = j // 3, j % 3
         for kk in (0, 1):
@@ -258,14 +259,15 @@
         turn(half, -1)
     group(1, ((0, 0), (1, 0), (-1, 0), (0, 1)))
     for half in both:
+        group(half, ((0, -1), (2, 0), (1, 1), (1, -1)))
+    for half in both:
         turn(half, 2)
     for half in both:
-        group(half, ((0, -1), (2, 0), (1, 1), (1, -1)))
-    for half in both:
-        group(half, ((-1, 1), (-1, -1), (2, 1), (2, -1)))
-    for half in both:
-        last(half, (0, 1, -1))
-        group(half, ((0, 2), (1, 2), (-1, 2)))
+        last(half, (0,))
+        group(half, ((-1, 1), (-1, -1), (0, 2), (2, 1)))
+    for half in both:
+        last(half, (1, -1))
+        group(half, ((2, -1), (1, 2), (-1, 2)))
     for half in both:
         last(half, (2,))
         group(half, ((2, 2),))
@@ -288,29 +290,34 @@
     for n in range(24):
         z = dot_nn(sketch_t[n % 6], total[n].astype(BF))
         sampled[n] = z
-        z2 = jnp.concatenate([z, z], axis=0)
-        gram = dot_nt(z, z2, precision=HIGH)
+        high = z.astype(BF)
+        rest = z - high.astype(F32)
+        mid = rest.astype(BF)
+        low = (rest - mid.astype(F32)).astype(BF)
+        one = jnp.concatenate([high, mid, high, low, mid, high], axis=1)
+        two = jnp.concatenate([high, high, mid, high, mid, low], axis=1)
+        gram = dot_nt(one, jnp.concatenate([two, two], axis=0))
         grams[pl.ds(n, 64, stride=24), :] = jnp.where(lane2 >= 64, gram, eye)
 
     for base in range(0, 64, PANEL):
         rows = [grams[24 * c : 24 * c + 24, :] for c in range(base, base + PANEL)]
-        for low in range(0, PANEL, 4):
+        for low in range(0, PANEL, 8):
 
             def entry(t, c):
                 at = 64 + base + low + c
                 return jnp.broadcast_to(rows[low + t][:, at : at + 1], (24, 128))
 
-            corner = {(t, c): entry(t, c) for t in range(4) for c in range(t, 4)}
-            for t in range(4):
+            corner = {(t, c): entry(t, c) for t in range(8) for c in range(t, 8)}
+            for t in range(8):
                 row = rows[low + t]
                 inverse = 1.0 / corner[t, t]
                 scaled = row * inverse
-                for u in range(t + 1, 4):
+                for u in range(t + 1, 8):
                     rows[low + u] = rows[low + u] - corner[t, u] * scaled
                     factor = corner[t, u] * inverse
-                    for c in range(u, 4):
+                    for c in range(u, 8):
                         corner[u, c] = corner[u, c] - factor * corner[t, c]
-                for u in range(low + 4, PANEL):
+                for u in range(low + 8, PANEL):
                     rows[u] = rows[u] - row[:, 64 + base + u : 65 + base + u] * scaled
                 rows[low + t] = row * lax.rsqrt(corner[t, t])
                 at = 24 * (base + low + t)

time: 92.5 us -> 91.9 us (level)
  no operation moved by 1% of the time
where the time goes in v4:
time: 91.9 us; the launch traced here: 90.7 us
  Pallas kernels  89.9 us (98%)
    pallas_call x1, Pallas kernels, per_device(): pl.pallas_call(kernel, name='gather_and_eliminate', out_shape=(jax.ShapeD...  87.4 us
    pallas_call x1, Pallas kernels, per_device(): pl.pallas_call(hand_over, name='hand_over', out_shape=(jax.ShapeDtypeStru...  2.47 us

profile of v4, /device:TPU:1, one launch (start us, length us, event | category | flops | bytes accessed | tf_op | source)
XLA Modules:
  0.0 90.7 jit_solution(5339361176943781565)
XLA Ops:
  0.6 87.4 %gather_and_eliminate.1 = (bf16[4,256,256]{2,1,0:T(8,128)(2,1)}, bf16[24,256,128]{2,1,0:T(8,128)(2,1)}) custom-call(s32[4]{0:T(128)} %bitcast.11, bf16[2,6,256,128]{3,2,1,0:T(8,128)(2,1)} %rows_hbm.1, bf16[4,4,256,128]{3,2,1,0:T(8,128)(2,1)} %panel_hbm.1, bf16[4,256,256]{2,1,0:T(8,128)(2,1)} %inv_hbm.1, bf16[24,256,128]{2,1,0:T(8,128)(2,1)} %bitcast.8, ...), custom_call_target="tpu_custom_call" | custom-call | tf_op jit(solution)/shard_map/gather_and_eliminate/pallas_call | solution.py:368
  88.1 2.5 %hand_over.1 = (bf16[4,256,256]{2,1,0:T(8,128)(2,1)}, bf16[24,256,128]{2,1,0:T(8,128)(2,1)}) custom-call(bf16[4,256,256]{2,1,0:T(8,128)(2,1)} %get-tuple-element.6.near_new, bf16[24,256,128]{2,1,0:T(8,128)(2,1)} %get-tuple-element.7.far_new), custom_call_target="tpu_custom_call" | custom-call | tf_op jit(solution)/shard_map/hand_over/pallas_call | solution.py:407
